TPU v7x, 32 devices: a whole 2x2x4 slice. The times are simulated.
32 devices in a mesh: groups: 2 (over y), leaf: 4 (over z), cols: 2 (over x), sub: 2 (over core).
Axes of the slice: x: 2, y: 2, z: 4, core: 2. Of those that a mesh axis runs over, the one named last changes fastest.
Arguments:
- right_side: float32 [512, 4, 768], P(('groups', 'cols'), 'leaf', 'sub'), parts along dimension 0, may hold values from -12 to 12
- leaf_diag: float32 [8, 768, 768], P(('groups', 'leaf'), 'sub'), parts along dimension 0, as said below
- leaf_rot: float32 [8, 768, 768], P(('groups', 'leaf'), 'sub'), parts along dimension 0, as said below
- node_rot: float32 [8, 768, 768], P(('groups', 'leaf'), 'sub'), parts along dimension 0, as said below
- coupling: float32 [8, 384, 384], P(('groups', 'leaf')), parts along dimension 0, may hold values from -0.15 to 0.15, as said below
- child_order: int32 [8], P(('groups', 'leaf')), parts along dimension 0, may hold values 0 or 1
Outputs:
- solution: float32 [512, 4, 768], P(('groups', 'cols'), 'leaf', 'sub'), parts along dimension 0
There are 2 independent parts, one for each index of `groups`. A program takes and returns all parts, laid end to end along the dimension named above; each array names one. Nothing has to cross between parts.
Inputs may be any that keep to these rules, and one draw needn't show every extreme that they name: `child_order`: entry g with 0 < g < 4 orders the children of the node at gap g; entry 0 belongs to no node. `leaf_diag`: every block is symmetric, with smallest eigenvalue at least 3. `leaf_rot`: every block is orthogonal up to rounding. `node_rot`: every block is orthogonal up to rounding; entry 0 belongs to no node. `coupling`: entry 0 belongs to no node.
All inputs are finite; a program needn't handle non-finite values. No bound on the sum of `child_order` on one device may be relied on, other than what follows from the above.
Results may differ from a plain program's by a relative error of at most 0.00013.
Values sent between devices are 32-bit elements; how exact they have to be, the bound alone decides.
A program may use at most 128 MiB of HBM per device.

v0:
```python
import functools

import jax
import jax.numpy as jnp
from jax import lax
from jax.experimental import pallas as pl
from jax.experimental.pallas import tpu as pltpu
from jax.sharding import PartitionSpec as P

f32 = jnp.float32
bf16 = jnp.bfloat16

VMEM_SPEC = pl.BlockSpec(memory_space=pltpu.VMEM)
SMEM_SPEC = pl.BlockSpec(memory_space=pltpu.SMEM)
NN = (((1,), (0,)), ((), ()))
NT = (((1,), (1,)), ((), ()))


def split(x):
    high = x.astype(bf16)
    return high, (x - high.astype(f32)).astype(bf16)


def one(a, b, dims=NN):
    return lax.dot_general(a, b, dims, preferred_element_type=f32)


def product(a, b, dims=NN):
    axis = dims[0][1][0]
    left = jnp.concatenate([a[0], a[1], a[0]], axis=1)
    return one(left, jnp.concatenate([b[0], b[0], b[1]], axis=axis), dims)


def eye(n):
    return (
        lax.broadcasted_iota(jnp.int32, (n, n), 0) == lax.broadcasted_iota(jnp.int32, (n, n), 1)
    ).astype(f32)


def invert(e_ref, x_ref, r_ref):
    n = e_ref.shape[0]
    e = e_ref[...]
    bound = jnp.max(jnp.sum(jnp.abs(e), axis=0, keepdims=True))
    scale = 1.9 / bound
    start = eye(n) - scale * e
    x_ref[...] = scale * (eye(n) + start)
    low = start.astype(bf16)
    first = one(low, low)
    r_ref[...] = first

    def rough_go(state):
        step, size = state
        return jnp.logical_and(step < 40, size > 4e-3)

    def rough(state):
        step, _ = state
        r = r_ref[...].astype(bf16)
        x = x_ref[...]
        both = one(jnp.concatenate([x.astype(bf16), r], axis=0), r)
        x_ref[...] = x + both[:n]
        squared = both[n:]
        r_ref[...] = squared
        return step + 1, jnp.sum(squared * squared)

    lax.while_loop(rough_go, rough, (jnp.int32(0), jnp.sum(first * first)))
    e_parts = split(e_ref[...])

    def residual():
        r = eye(n) - product(e_parts, split(x_ref[...]))
        r_ref[...] = r
        return jnp.sum(r * r)

    size = residual()
    restart = jnp.logical_not(size < 0.25)

    @pl.when(restart)
    def _():
        x_ref[...] = scale * eye(n)
        residual()

    def fine_go(state):
        step, now, before = state
        stalled = jnp.logical_and(before < 1e-2, now > 0.5 * before)
        more = jnp.logical_and(now > 1e-10, jnp.logical_not(stalled))
        return jnp.logical_and(step < 64, more)

    def fine(state):
        step, now, _ = state
        x = x_ref[...]
        small = now < 1e-6
        r = r_ref[...]

        @pl.when(now < 1e-2)
        def _():
            x_ref[...] = x + one(x.astype(bf16), r.astype(bf16))

        @pl.when(jnp.logical_not(now < 1e-2))
        def _():
            x_ref[...] = x + product(split(x), split(r))

        after = lax.cond(small, lambda: jnp.float32(0.0), residual)
        return step + 1, after, now

    lax.while_loop(
        fine_go, fine, (jnp.int32(0), jnp.where(restart, jnp.float32(1e6), size), jnp.float32(1e9))
    )


def wide_product(a, b, store):
    full = b[0].shape[1]
    width = 256 if full % 256 == 0 else full

    def block(j, carry):
        columns = pl.ds(pl.multiple_of(j * width, width), width)
        store(columns, product((a[0][...], a[1][...]), (b[0][:, columns], b[1][:, columns])))
        return carry

    lax.fori_loop(0, full // width, block, 0)


def eliminate(a, q, qt, b, p, t_ref, e_ref, m_ref, r_ref):
    n = e_ref.shape[0]

    def store_p(columns, value):
        p[0][:, columns], p[1][:, columns] = split(value)

    full_width = t_ref.shape[0]
    wide_product(a, q, store_p)
    width = full_width // 3
    for j in range(3):
        below, columns = slice(0, (j + 1) * width), slice(j * width, (j + 1) * width)
        t_ref[below, columns] = product(
            (qt[0][below, :], qt[1][below, :]), (p[0][:, columns], p[1][:, columns])
        )
    t_ref[width:n, :width] = t_ref[:width, width:n].T
    t_ref[2 * width :, n : 2 * width] = t_ref[n : 2 * width, 2 * width :].T
    e_ref[...] = t_ref[:n, :n]
    invert(e_ref, m_ref, r_ref)
    c = t_ref[:n, n:]
    g = product(split(m_ref[...]), split(c))
    g_parts = split(g)
    schur = t_ref[n:, n:] - product(split(c.T), g_parts)
    bq = product(b, (q[0][...], q[1][...]))
    be = bq[:, :n]
    carried = bq[:, n:] - product(split(be), g_parts)
    return schur, carried, g, be


def load_rotation(sub, q_own, q_oth, q, qt):
    n = q_own.shape[0]
    for which, ref in ((sub, q_own), (1 - sub, q_oth)):
        rows = pl.ds(pl.multiple_of(which * n, n), n)
        high, low = split(ref[...])
        q[0][rows, :] = high
        q[1][rows, :] = low
    if qt is not None:
        qt[0][...] = q[0][...].T
        qt[1][...] = q[1][...].T


def pack(sub, s_ref, c, out):
    n = s_ref.shape[0]
    b = n // 3

    @pl.when(sub == 0)
    def _():
        out[:n, :] = s_ref[:, :b]

    @pl.when(sub != 0)
    def _():
        out[: 2 * b, :] = s_ref[b:, b : 2 * b]
        out[2 * b : n, :] = s_ref[2 * b :, 2 * b :]

    count = c.shape[0]
    for j in range(3):
        out[n + j * count : n + (j + 1) * count, :] = c[:, j * b : (j + 1) * b]


def unpack(sub, own, oth):
    b = own.shape[1]
    n = 3 * b
    one_, two = by_half(sub, own[:n, :], oth[:n, :])
    top = jnp.concatenate([one_[:b], one_[b : 2 * b].T, one_[2 * b :].T], axis=1)
    mid = jnp.concatenate([one_[b : 2 * b], two[:b], two[b : 2 * b].T], axis=1)
    end = jnp.concatenate([one_[2 * b :], two[b : 2 * b], two[2 * b :]], axis=1)
    count = (own.shape[0] - n) // 3
    c = jnp.concatenate([own[n + j * count : n + (j + 1) * count, :] for j in range(3)], axis=1)
    return jnp.concatenate([top, mid, end], axis=0), c


def by_half(sub, own, oth):
    first = sub == 0
    return jnp.where(first, own, oth), jnp.where(first, oth, own)


def recover(be, m, g, x, q):
    w = product(split(be), split(m)) - product(split(x), split(g), NT)
    return product(split(jnp.concatenate([w, x], axis=1)), (q[0][...], q[1][...]), NT)


def leaf_kernel(
    flags, a_own, a_oth, q_own, q_oth, b_own, b_oth,
    s_out, load_out, c_out, m_out, g_out, be_out,
    ah, al, qh, ql, qth, qtl, ph, pl_, t_ref, e_ref, r_ref,
):
    sub = flags[0]
    load_rotation(sub, a_own, a_oth, (ah, al), None)
    load_rotation(sub, q_own, q_oth, (qh, ql), (qth, qtl))
    b = jnp.concatenate(by_half(sub, b_own[...], b_oth[...]), axis=1)
    s, c, g, be = eliminate(
        (ah, al), (qh, ql), (qth, qtl), split(b), (ph, pl_), t_ref, e_ref, m_out, r_ref
    )
    s_out[...] = s
    pack(sub, s_out, c, load_out)
    c_out[...] = c
    g_out[...] = g
    be_out[...] = be


def node_kernel(is_root, right_whole, *refs):
    flags, l_own, l_oth = refs[:3]
    refs = refs[3:]
    if right_whole:
        (r_whole, r_carried), refs = refs[:2], refs[2:]
    else:
        (r_own, r_oth), refs = refs[:2], refs[2:]
    (coup, q_own, q_oth), refs = refs[:3], refs[3:]
    if is_root:
        (left_out, right_out), refs = refs[:2], refs[2:]
        (x_ref, g_ref, s_ref, minv_ref), refs = refs[:4], refs[4:]
    else:
        (load_out, x_ref, g_ref, be_out), refs = refs[:4], refs[4:]
        (s_ref,), refs = refs[:1], refs[1:]
    ah, al, qh, ql, qth, qtl, ph, pl_, t_ref, e_ref, r_ref = refs
    sub = flags[0]
    n = e_ref.shape[0]

    @pl.when(flags[1] != 0)
    def _():
        load_rotation(sub, q_own, q_oth, (qh, ql), (qth, qtl))
        flipped = flags[2] != 0
        left, cl = unpack(sub, l_own, l_oth)
        if right_whole:
            right, cr = r_whole[...], r_carried[...]
        else:
            right, cr = unpack(sub, r_own, r_oth)
        coupling = coup[...]
        for row, col, value in (
            (0, 0, jnp.where(flipped, right, left)),
            (0, n, coupling),
            (n, 0, coupling.T),
            (n, n, jnp.where(flipped, left, right)),
        ):
            high, low = split(value)
            ah[row : row + n, col : col + n] = high
            al[row : row + n, col : col + n] = low
        b = jnp.concatenate(
            [jnp.where(flipped, cr, cl), jnp.where(flipped, cl, cr)], axis=1
        )
        s, c, g, be = eliminate(
            (ah, al), (qh, ql), (qth, qtl), split(b), (ph, pl_), t_ref, e_ref, x_ref, r_ref
        )
        s_ref[...] = s
        g_ref[...] = g
        if is_root:
            invert(s_ref, minv_ref, r_ref)
            x = product(split(c), split(minv_ref[...]))
            v = recover(be, x_ref[...], g_ref[...], x, (qh, ql))
            left_out[...] = jnp.where(flipped, v[:, n:], v[:, :n])
            right_out[...] = jnp.where(flipped, v[:, :n], v[:, n:])
        else:
            pack(sub, s_ref, c, load_out)
            be_out[...] = be


def down_kernel(flags, be, m, g, xa, xb, q_own, q_oth, left_out, right_out, qh, ql):
    sub = flags[0]
    n = m.shape[0]

    @pl.when(flags[1] != 0)
    def _():
        load_rotation(sub, q_own, q_oth, (qh, ql), None)
        x = jnp.where(flags[3] != 0, xa[...], xb[...])
        v = recover(be[...], m[...], g[...], x, (qh, ql))
        flipped = flags[2] != 0
        left_out[...] = jnp.where(flipped, v[:, n:], v[:, :n])
        right_out[...] = jnp.where(flipped, v[:, :n], v[:, n:])


def shape(*dims):
    return jax.ShapeDtypeStruct(dims, f32)


def call(kernel, outs, scratch, args, name):
    return pl.pallas_call(
        kernel,
        out_shape=outs,
        in_specs=[SMEM_SPEC] + [VMEM_SPEC] * (len(args) - 1),
        out_specs=jax.tree.map(lambda _: VMEM_SPEC, outs),
        scratch_shapes=scratch,
        compiler_params=pltpu.CompilerParams(vmem_limit_bytes=36 * 2**20),
        name=name,
    )(*args)


def swap(value):
    return lax.ppermute(value, "sub", [(0, 1), (1, 0)])


def hop(value, pairs):
    return lax.ppermute(value, "leaf", pairs)


def local(right_side, leaf_diag, leaf_rot, node_rot, coupling, child_order):
    sub = lax.axis_index("sub")
    pos = lax.axis_index("leaf")
    leaves = lax.axis_size("leaf")
    levels = leaves.bit_length() - 1
    full = leaf_diag.shape[-1]
    n = coupling.shape[-1]
    count = right_side.shape[0] // 2
    load = (n + 3 * count, n // 3)

    b_all = right_side[:, 0, :]
    b_own = lax.dynamic_slice_in_dim(b_all, sub * count, count, 0)
    b_oth = swap(lax.dynamic_slice_in_dim(b_all, (1 - sub) * count, count, 0))
    q_own, a_own, r_own = leaf_rot[0], leaf_diag[0], node_rot[0]
    q_oth, a_oth, r_oth = swap(q_own), swap(a_own), swap(r_own)
    flip = child_order[0]

    def flags(active, choice):
        return jnp.stack(
            [sub.astype(jnp.int32), active.astype(jnp.int32), flip, choice.astype(jnp.int32)]
        )

    always = jnp.ones((), jnp.int32)
    big = [pltpu.VMEM((full, full), bf16)] * 8
    small = [pltpu.VMEM((full, full), f32)] + [pltpu.VMEM((n, n), f32)] * 2
    schur, payload, carried, m_leaf, g_leaf, be_leaf = call(
        leaf_kernel,
        (shape(n, n), shape(*load), shape(count, n), shape(n, n), shape(n, n), shape(count, n)),
        big + small,
        (flags(always, always), a_own, a_oth, q_own, q_oth, b_own, b_oth),
        "leaf_up",
    )
    kept = {}
    for level in range(1, levels + 1):
        span = 2 ** (level - 1)
        gaps = range(span, leaves, 2 * span)
        owner = pos % (2 * span) == span
        step = max(span // 2, 1)
        to_right = [(g - step, g) for g in gaps]
        l_own = hop(payload, to_right)
        if level == 1:
            right = (schur, carried)
        else:
            to_left = [(g + step, g) for g in gaps]
            got = hop(payload, to_left)
            right = (got, swap(got))
        is_root = level == levels
        args = (flags(owner, always), l_own, swap(l_own), *right, coupling[0], r_own, r_oth)
        body = functools.partial(node_kernel, is_root, level == 1)
        if is_root:
            left_x, right_x = call(
                body, (shape(count, n), shape(count, n)),
                [pltpu.VMEM((n, n), f32)] * 4 + big + small, args, "root",
            )
        else:
            payload, m_node, g_node, be_node = call(
                body,
                (shape(*load), shape(n, n), shape(n, n), shape(count, n)),
                [pltpu.VMEM((n, n), f32)] + big + small, args, "node_up",
            )
            kept[level] = (be_node, m_node, g_node)
    turn = [pltpu.VMEM((full, full), bf16)] * 2
    for level in range(levels, 0, -1):
        span = 2 ** (level - 1)
        gaps = range(span, leaves, 2 * span)
        if level < levels:
            owner = pos % (2 * span) == span
            left_x, right_x = call(
                down_kernel,
                (shape(count, n), shape(count, n)),
                turn,
                (flags(owner, choice), *kept[level], got_left, got_right, r_own, r_oth),
                "node_down",
            )
        if level == 1:
            got_left = hop(left_x, [(g, g - 1) for g in gaps])
            got_right = right_x
            choice = pos % 2 == 0
        else:
            step = span // 2
            got_left = hop(left_x, [(g, g - step) for g in gaps])
            got_right = hop(right_x, [(g, g + step) for g in gaps])
            choice = pos // span % 2 == 0
    first, second = call(
        down_kernel,
        (shape(count, n), shape(count, n)),
        turn,
        (
            jnp.stack([sub.astype(jnp.int32), always, sub.astype(jnp.int32), choice.astype(jnp.int32)]),
            be_leaf, m_leaf, g_leaf, got_left, got_right, q_own, q_oth,
        ),
        "leaf_down",
    )
    received = swap(second)
    out = jnp.where(
        sub == 0,
        jnp.concatenate([first, received], axis=0),
        jnp.concatenate([received, first], axis=0),
    )
    return out[:, None, :]


def solution(mesh):
    placed = (
        P(("groups", "cols"), "leaf", "sub"),
        P(("groups", "leaf"), "sub", None),
        P(("groups", "leaf"), "sub", None),
        P(("groups", "leaf"), "sub", None),
        P(("groups", "leaf"), None, None),
        P(("groups", "leaf")),
    )
    return jax.shard_map(
        local,
        mesh=mesh,
        in_specs=placed,
        out_specs=P(("groups", "cols"), "leaf", "sub"),
        check_vma=False,
    )
```

profile of v0, /device:TPU:0, one launch (start us, length us, event | category | flops | bytes accessed | tf_op | source)
XLA Modules:
  0.0 126.1 jit_solution(16749013355834808704)
XLA Ops:
  0.0 0.5 collective-permute-start
  0.5 0.0 collective-permute-start.1
  0.5 0.5 collective-permute-start.5
  1.0 1.0 constant_dynamic-slice_fusion
  2.1 0.1 collective-permute-start.2
  2.8 0.1 pad_add_fusion.2.flags
  2.9 3.8 %collective-permute-done.2.b_oth = f32[64,384]{1,0:T(8,128)S(1)} collective-permute-done((f32[64,384]{1,0:T(8,128)S(1)}, f32[64,384]{1,0:T(8,128)S(1)}, u32[]{:S(2)}, u32[]{:S(2)}) %collective-permute-start.2) | collective-permute-done | bytes 98336 | tf_op jit(solution)/shard_map/ppermute | solution.py:307
  6.7 0.0 collective-permute-done.a_oth
  6.7 1.0 copy-done.6
  7.7 0.0 collective-permute-done.1.q_oth
  7.7 1.3 %copy-done.1 = f32[1,384,768]{2,1,0:T(8,128)S(1)} copy-done((f32[1,384,768]{2,1,0:T(8,128)S(1)}, f32[1,384,768]{2,1,0:T(8,128)}, u32[]{:S(2)}) %copy-start.1) | copy-done | bytes 1179672
  9.0 1.3 %copy-done.5 = f32[1,384,768]{2,1,0:T(8,128)S(1)} copy-done((f32[1,384,768]{2,1,0:T(8,128)S(1)}, f32[1,384,768]{2,1,0:T(8,128)}, u32[]{:S(2)}) %copy-start.5) | copy-done | bytes 1179672
  10.3 1.3 %copy-done.7 = f32[384,768]{1,0:T(8,128)S(1)} copy-done((f32[384,768]{1,0:T(8,128)S(1)}, f32[384,768]{1,0:T(8,128)}, u32[]{:S(2)}) %copy-start.7) | copy-done | bytes 1179672
  11.6 15.7 %leaf_up.1 = (f32[384,384]{1,0:T(8,128)S(1)}, f32[576,128]{1,0:T(8,128)S(1)}, f32[64,384]{1,0:T(8,128)S(1)}, f32[384,384]{1,0:T(8,128)S(1)}, f32[384,384]{1,0:T(8,128)S(1)}, /*index=5*/f32[64,384]{1,0:T(8,128)S(1)}) custom-call(s32[4]{0:T(128)S(1)} %pad_add_fusion.2.flags, f32[384,768]{1,0:T(8,128)S(1)} %bitcast.27, f32[384,768]{1,0:T(8,128)S(1)} %copy-done.7, ...), custom_call_target="tpu_custom_call" | custom-call | tf_op jit(solution)/shard_map/leaf_up/pallas_call | solution.py:295
  27.2 0.0 copy-start.8
  27.3 0.8 copy-done.8
  28.1 0.8 copy-done.10
  28.9 0.8 copy-done.12
  29.7 0.6 copy-done.18
  30.4 0.6 copy-done.22
  31.0 5.6 %collective-permute-start.3 = (f32[576,128]{1,0:T(8,128)S(1)}, f32[576,128]{1,0:T(8,128)}, u32[]{:S(2)}, u32[]{:S(2)}) collective-permute-start(f32[576,128]{1,0:T(8,128)S(1)} %get-tuple-element.24), channel_id=1, source_target_pairs={{0,4},{8,12},{1,5},{9,13},{2,6},{10,14},{3,7},{11,15},{16,20},{24,... | collective-permute-start | bytes 884744 | tf_op jit(solution)/shard_map/ppermute | solution.py:311
  36.6 5.8 %collective-permute-done.3.refs_1_ = f32[576,128]{1,0:T(8,128)} collective-permute-done((f32[576,128]{1,0:T(8,128)S(1)}, f32[576,128]{1,0:T(8,128)}, u32[]{:S(2)}, u32[]{:S(2)}) %collective-permute-start.3) | collective-permute-done | bytes 294944 | tf_op jit(solution)/shard_map/ppermute | solution.py:311
  42.4 0.0 collective-permute-start.4
  42.4 0.1 pad_add_fusion.1
  42.5 0.0 collective-permute-done.5.refs_7_.q_oth
  42.5 1.8 %collective-permute-done.4.refs_2_ = f32[576,128]{1,0:T(8,128)} collective-permute-done((f32[576,128]{1,0:T(8,128)}, f32[576,128]{1,0:T(8,128)}, u32[]{:S(2)}, u32[]{:S(2)}) %collective-permute-start.4) | collective-permute-done | bytes 294944 | tf_op jit(solution)/shard_map/ppermute | solution.py:307
  44.3 0.0 copy-done
  44.3 1.1 copy-done.3
  45.4 1.1 copy-done.9
  46.5 0.9 copy-done.23
  47.4 1.3 %node_up.1 = (f32[576,128]{1,0:T(8,128)S(1)}, f32[384,384]{1,0:T(8,128)S(1)}, f32[384,384]{1,0:T(8,128)S(1)}, f32[64,384]{1,0:T(8,128)S(1)}) custom-call(s32[4]{0:T(128)S(1)} %get-tuple-element.37.refs_0_, f32[576,128]{1,0:T(8,128)} %collective-permute-done.3.refs_1_, f32[576,128]{1,0:T(8,128)} %collective-permute-done.4.refs_2_, f32[384,384]{1,0:T(8,128)S(1)} %copy-done.9, ...), custom_call_target="tpu_custom_call" | custom-call | tf_op jit(solution)/shard_map/node_up/pallas_call | solution.py:295
  48.7 0.0 copy-start.14
  48.7 0.8 copy-done.14
  49.5 0.8 copy-done.16
  50.3 0.6 copy-done.20
  50.9 1.4 %collective-permute-start.8 = (f32[576,128]{1,0:T(8,128)S(1)}, f32[576,128]{1,0:T(8,128)}, u32[]{:S(2)}, u32[]{:S(2)}) collective-permute-start(f32[576,128]{1,0:T(8,128)S(1)} %get-tuple-element.30), channel_id=1, source_target_pairs={{12,8},{13,9},{14,10},{15,11},{28,24},{29,25},{30,26},{31,27}} | collective-permute-start | bytes 884744 | tf_op jit(solution)/shard_map/ppermute | solution.py:311
  52.3 1.4 %collective-permute-start.6 = (f32[576,128]{1,0:T(8,128)S(1)}, f32[576,128]{1,0:T(8,128)}, u32[]{:S(2)}, u32[]{:S(2)}) collective-permute-start(f32[576,128]{1,0:T(8,128)S(1)} %get-tuple-element.30), channel_id=1, source_target_pairs={{4,8},{5,9},{6,10},{7,11},{20,24},{21,25},{22,26},{23,27}} | collective-permute-start | bytes 884744 | tf_op jit(solution)/shard_map/ppermute | solution.py:311
  53.7 0.0 collective-permute-done.8.refs_3_
  53.7 0.1 collective-permute-start.9
  53.8 0.0 collective-permute-done.6.refs_1_
  53.9 0.4 collective-permute-start.7
  54.2 0.1 pad_add_fusion.refs_0_
  54.3 1.3 %collective-permute-done.9.refs_4_ = f32[576,128]{1,0:T(8,128)} collective-permute-done((f32[576,128]{1,0:T(8,128)}, f32[576,128]{1,0:T(8,128)}, u32[]{:S(2)}, u32[]{:S(2)}) %collective-permute-start.9) | collective-permute-done | bytes 294944 | tf_op jit(solution)/shard_map/ppermute | solution.py:307
  55.6 0.4 collective-permute-done.7.refs_2_
  56.1 1.1 copy-done.4
  57.1 2.2 %root.1 = (f32[64,384]{1,0:T(8,128)}, f32[64,384]{1,0:T(8,128)}) custom-call(s32[4]{0:T(128)S(1)} %pad_add_fusion.refs_0_, f32[576,128]{1,0:T(8,128)} %collective-permute-done.6.refs_1_, f32[576,128]{1,0:T(8,128)} %collective-permute-done.7.refs_2_, f32[576,128]{1,0:T(8,128)} %collective-permute-done.8.refs_3_, f32[576,128]{1,0:T(8,128)} %collective-permute-done.9.refs_4_, ...), custom_call_target="tpu_custom_call" | custom-call | tf_op jit(solution)/shard_map/root/pallas_call | solution.py:295
  59.3 1.3 %collective-permute-start.10 = (f32[64,384]{1,0:T(8,128)}, f32[64,384]{1,0:T(8,128)}, u32[]{:S(2)}, u32[]{:S(2)}) collective-permute-start(f32[64,384]{1,0:T(8,128)} %get-tuple-element.31), channel_id=1, source_target_pairs={{8,4},{9,5},{10,6},{11,7},{24,20},{25,21},{26,22},{27,23}} | collective-permute-start | bytes 294920 | tf_op jit(solution)/shard_map/ppermute | solution.py:311
  60.6 1.3 %collective-permute-start.11 = (f32[64,384]{1,0:T(8,128)}, f32[64,384]{1,0:T(8,128)}, u32[]{:S(2)}, u32[]{:S(2)}) collective-permute-start(f32[64,384]{1,0:T(8,128)} %get-tuple-element.32), channel_id=1, source_target_pairs={{8,12},{9,13},{10,14},{11,15},{24,28},{25,29},{26,30},{27,31}} | collective-permute-start | bytes 294920 | tf_op jit(solution)/shard_map/ppermute | solution.py:311
  61.9 0.1 pad_add_fusion.5.flags
  62.0 0.0 collective-permute-done.10.xa
  62.0 0.0 collective-permute-done.11.xb
  62.0 1.1 copy-done.15
  63.1 1.1 copy-done.17
  64.2 0.9 copy-done.21
  65.1 1.1 node_down.1
  66.2 1.3 %collective-permute-start.12 = (f32[64,384]{1,0:T(8,128)S(1)}, f32[64,384]{1,0:T(8,128)S(1)}, u32[]{:S(2)}, u32[]{:S(2)}) collective-permute-start(f32[64,384]{1,0:T(8,128)S(1)} %get-tuple-element.33), channel_id=1, source_target_pairs={{4,0},{12,8},{5,1},{13,9},{6,2},{14,10},{7,3},{15,11},{20,16},{28,... | collective-permute-start | bytes 294920 | tf_op jit(solution)/shard_map/ppermute | solution.py:311
  67.5 0.1 pad_add_fusion.3.flags
  67.6 53.6 %collective-permute-done.12.xa = f32[64,384]{1,0:T(8,128)S(1)} collective-permute-done((f32[64,384]{1,0:T(8,128)S(1)}, f32[64,384]{1,0:T(8,128)S(1)}, u32[]{:S(2)}, u32[]{:S(2)}) %collective-permute-start.12) | collective-permute-done | bytes 98336 | tf_op jit(solution)/shard_map/ppermute | solution.py:311
  121.1 0.0 copy-done.2
  121.1 0.0 copy-done.11
  121.1 2.6 %leaf_down.1 = (f32[64,384]{1,0:T(8,128)S(1)}, f32[64,384]{1,0:T(8,128)S(1)}) custom-call(s32[4]{0:T(128)S(1)} %pad_add_fusion.3.flags, f32[64,384]{1,0:T(8,128)S(1)} %copy-done.19, f32[384,384]{1,0:T(8,128)S(1)} %copy-done.11, f32[384,384]{1,0:T(8,128)S(1)} %copy-done.13, f32[64,384]{1,0:T(8,128)S(1)} %collective-permute-done.12.xa, ...), custom_call_target="tpu_custom_call" | custom-call | tf_op jit(solution)/shard_map/leaf_down/pallas_call | solution.py:295
  123.8 0.1 collective-permute-start.13
  123.9 1.3 %collective-permute-done.13 = f32[64,384]{1,0:T(8,128)S(1)} collective-permute-done((f32[64,384]{1,0:T(8,128)S(1)}, f32[64,384]{1,0:T(8,128)S(1)}, u32[]{:S(2)}, u32[]{:S(2)}) %collective-permute-start.13) | collective-permute-done | bytes 98336 | tf_op jit(solution)/shard_map/ppermute | solution.py:307
  125.2 0.9 copy.7
  (27 shorter events, 0.1 us)
Async XLA Ops:
  0.0 6.7 %collective-permute-start = (f32[384,768]{1,0:T(8,128)}, f32[384,768]{1,0:T(8,128)S(1)}, u32[]{:S(2)}, u32[]{:S(2)}) collective-permute-start(f32[384,768]{1,0:T(8,128)} %bitcast.26), channel_id=1, source_target_pairs={{0,1},{1,0},{2,3},{3,2},{4,5},{5,4},{6,7},{7,6},{8,9},{9,8},{10,11... | collective-permute-start | bytes 3538952 | tf_op jit(solution)/shard_map/ppermute | solution.py:307
  0.5 7.2 %collective-permute-start.1 = (f32[384,768]{1,0:T(8,128)}, f32[384,768]{1,0:T(8,128)S(1)}, u32[]{:S(2)}, u32[]{:S(2)}) collective-permute-start(f32[384,768]{1,0:T(8,128)} %bitcast.21), channel_id=1, source_target_pairs={{0,1},{1,0},{2,3},{3,2},{4,5},{5,4},{6,7},{7,6},{8,9},{9,8},{10,11... | collective-permute-start | bytes 3538952 | tf_op jit(solution)/shard_map/ppermute | solution.py:307
  0.5 42.0 %collective-permute-start.5 = (f32[384,768]{1,0:T(8,128)}, f32[384,768]{1,0:T(8,128)S(1)}, u32[]{:S(2)}, u32[]{:S(2)}) collective-permute-start(f32[384,768]{1,0:T(8,128)} %bitcast.17), channel_id=1, source_target_pairs={{0,1},{1,0},{2,3},{3,2},{4,5},{5,4},{6,7},{7,6},{8,9},{9,8},{10,11... | collective-permute-start | bytes 3538952 | tf_op jit(solution)/shard_map/ppermute | solution.py:307
  2.1 4.6 %collective-permute-start.2 = (f32[64,384]{1,0:T(8,128)S(1)}, f32[64,384]{1,0:T(8,128)S(1)}, u32[]{:S(2)}, u32[]{:S(2)}) collective-permute-start(f32[64,384]{1,0:T(8,128)S(1)} %bitcast.30), channel_id=1, source_target_pairs={{0,1},{1,0},{2,3},{3,2},{4,5},{5,4},{6,7},{7,6},{8,9},{9,8},{10,11... | collective-permute-start | bytes 294920 | tf_op jit(solution)/shard_map/ppermute | solution.py:307
  6.7 1.0 copy-start.6
  7.7 1.3 %copy-start.1 = (f32[1,384,768]{2,1,0:T(8,128)S(1)}, f32[1,384,768]{2,1,0:T(8,128)}, u32[]{:S(2)}) copy-start(f32[1,384,768]{2,1,0:T(8,128)} %param.8) | copy-start | bytes 3538948
  9.0 1.3 %copy-start.5 = (f32[1,384,768]{2,1,0:T(8,128)S(1)}, f32[1,384,768]{2,1,0:T(8,128)}, u32[]{:S(2)}) copy-start(f32[1,384,768]{2,1,0:T(8,128)} %param.7) | copy-start | bytes 3538948
  10.3 1.3 %copy-start.7 = (f32[384,768]{1,0:T(8,128)S(1)}, f32[384,768]{1,0:T(8,128)}, u32[]{:S(2)}) copy-start(f32[384,768]{1,0:T(8,128)} %copy-done.6) | copy-start | bytes 3538948
  11.6 32.8 %copy-start = (f32[1,384,768]{2,1,0:T(8,128)S(1)}, f32[1,384,768]{2,1,0:T(8,128)}, u32[]{:S(2)}) copy-start(f32[1,384,768]{2,1,0:T(8,128)} %param.9) | copy-start | bytes 3538948
  27.2 0.8 copy-start.8
  28.1 0.8 copy-start.10
  28.9 0.8 copy-start.12
  29.7 0.6 copy-start.18
  30.4 0.6 copy-start.22
  31.0 11.4 %collective-permute-start.3 = (f32[576,128]{1,0:T(8,128)S(1)}, f32[576,128]{1,0:T(8,128)}, u32[]{:S(2)}, u32[]{:S(2)}) collective-permute-start(f32[576,128]{1,0:T(8,128)S(1)} %get-tuple-element.24), channel_id=1, source_target_pairs={{0,4},{8,12},{1,5},{9,13},{2,6},{10,14},{3,7},{11,15},{16,20},{24,... | collective-permute-start | bytes 884744 | tf_op jit(solution)/shard_map/ppermute | solution.py:311
  42.4 1.9 %collective-permute-start.4 = (f32[576,128]{1,0:T(8,128)}, f32[576,128]{1,0:T(8,128)}, u32[]{:S(2)}, u32[]{:S(2)}) collective-permute-start(f32[576,128]{1,0:T(8,128)} %collective-permute-done.3.refs_1_), channel_id=1, source_target_pairs={{0,1},{1,0},{2,3},{3,2},{4,5},{5,4},{6,7},{7,6},{8,9},{9,8},{10,11... | collective-permute-start | bytes 884744 | tf_op jit(solution)/shard_map/ppermute | solution.py:307
  44.3 1.1 copy-start.3
  45.4 1.1 copy-start.9
  46.5 0.9 copy-start.23
  48.7 0.8 copy-start.14
  49.5 0.8 copy-start.16
  50.3 0.6 copy-start.20
  50.9 2.8 %collective-permute-start.8 = (f32[576,128]{1,0:T(8,128)S(1)}, f32[576,128]{1,0:T(8,128)}, u32[]{:S(2)}, u32[]{:S(2)}) collective-permute-start(f32[576,128]{1,0:T(8,128)S(1)} %get-tuple-element.30), channel_id=1, source_target_pairs={{12,8},{13,9},{14,10},{15,11},{28,24},{29,25},{30,26},{31,27}} | collective-permute-start | bytes 884744 | tf_op jit(solution)/shard_map/ppermute | solution.py:311
  52.3 1.5 %collective-permute-start.6 = (f32[576,128]{1,0:T(8,128)S(1)}, f32[576,128]{1,0:T(8,128)}, u32[]{:S(2)}, u32[]{:S(2)}) collective-permute-start(f32[576,128]{1,0:T(8,128)S(1)} %get-tuple-element.30), channel_id=1, source_target_pairs={{4,8},{5,9},{6,10},{7,11},{20,24},{21,25},{22,26},{23,27}} | collective-permute-start | bytes 884744 | tf_op jit(solution)/shard_map/ppermute | solution.py:311
  53.7 1.9 %collective-permute-start.9 = (f32[576,128]{1,0:T(8,128)}, f32[576,128]{1,0:T(8,128)}, u32[]{:S(2)}, u32[]{:S(2)}) collective-permute-start(f32[576,128]{1,0:T(8,128)} %collective-permute-done.8.refs_3_), channel_id=1, source_target_pairs={{0,1},{1,0},{2,3},{3,2},{4,5},{5,4},{6,7},{7,6},{8,9},{9,8},{10,11... | collective-permute-start | bytes 884744 | tf_op jit(solution)/shard_map/ppermute | solution.py:307
  53.9 2.2 %collective-permute-start.7 = (f32[576,128]{1,0:T(8,128)}, f32[576,128]{1,0:T(8,128)}, u32[]{:S(2)}, u32[]{:S(2)}) collective-permute-start(f32[576,128]{1,0:T(8,128)} %collective-permute-done.6.refs_1_), channel_id=1, source_target_pairs={{0,1},{1,0},{2,3},{3,2},{4,5},{5,4},{6,7},{7,6},{8,9},{9,8},{10,11... | collective-permute-start | bytes 884744 | tf_op jit(solution)/shard_map/ppermute | solution.py:307
  56.1 1.1 copy-start.4
  59.3 2.7 %collective-permute-start.10 = (f32[64,384]{1,0:T(8,128)}, f32[64,384]{1,0:T(8,128)}, u32[]{:S(2)}, u32[]{:S(2)}) collective-permute-start(f32[64,384]{1,0:T(8,128)} %get-tuple-element.31), channel_id=1, source_target_pairs={{8,4},{9,5},{10,6},{11,7},{24,20},{25,21},{26,22},{27,23}} | collective-permute-start | bytes 294920 | tf_op jit(solution)/shard_map/ppermute | solution.py:311
  60.6 1.4 %collective-permute-start.11 = (f32[64,384]{1,0:T(8,128)}, f32[64,384]{1,0:T(8,128)}, u32[]{:S(2)}, u32[]{:S(2)}) collective-permute-start(f32[64,384]{1,0:T(8,128)} %get-tuple-element.32), channel_id=1, source_target_pairs={{8,12},{9,13},{10,14},{11,15},{24,28},{25,29},{26,30},{27,31}} | collective-permute-start | bytes 294920 | tf_op jit(solution)/shard_map/ppermute | solution.py:311
  62.0 1.1 copy-start.15
  63.1 1.1 copy-start.17
  64.2 0.9 copy-start.21
  65.0 56.1 %copy-start.2 = (f32[1,384,768]{2,1,0:T(8,128)S(1)}, f32[1,384,768]{2,1,0:T(8,128)}, u32[]{:S(2)}) copy-start(f32[1,384,768]{2,1,0:T(8,128)} %param.8) | copy-start | bytes 3538948
  65.0 56.1 %copy-start.11 = (f32[384,384]{1,0:T(8,128)S(1)}, f32[384,384]{1,0:T(8,128)}, u32[]{:S(2)}) copy-start(f32[384,384]{1,0:T(8,128)} %copy-done.10) | copy-start | bytes 1769476
  65.0 56.1 %copy-start.13 = (f32[384,384]{1,0:T(8,128)S(1)}, f32[384,384]{1,0:T(8,128)}, u32[]{:S(2)}) copy-start(f32[384,384]{1,0:T(8,128)} %copy-done.12) | copy-start | bytes 1769476
  65.1 56.1 %copy-start.19 = (f32[64,384]{1,0:T(8,128)S(1)}, f32[64,384]{1,0:T(8,128)}, u32[]{:S(2)}) copy-start(f32[64,384]{1,0:T(8,128)} %copy-done.18) | copy-start | bytes 294916
  66.2 54.9 %collective-permute-start.12 = (f32[64,384]{1,0:T(8,128)S(1)}, f32[64,384]{1,0:T(8,128)S(1)}, u32[]{:S(2)}, u32[]{:S(2)}) collective-permute-start(f32[64,384]{1,0:T(8,128)S(1)} %get-tuple-element.33), channel_id=1, source_target_pairs={{4,0},{12,8},{5,1},{13,9},{6,2},{14,10},{7,3},{15,11},{20,16},{28,... | collective-permute-start | bytes 294920 | tf_op jit(solution)/shard_map/ppermute | solution.py:311
  123.8 1.4 %collective-permute-start.13 = (f32[64,384]{1,0:T(8,128)S(1)}, f32[64,384]{1,0:T(8,128)S(1)}, u32[]{:S(2)}, u32[]{:S(2)}) collective-permute-start(f32[64,384]{1,0:T(8,128)S(1)} %get-tuple-element.36), channel_id=1, source_target_pairs={{0,1},{1,0},{2,3},{3,2},{4,5},{5,4},{6,7},{7,6},{8,9},{9,8},{10,11... | collective-permute-start | bytes 294920 | tf_op jit(solution)/shard_map/ppermute | solution.py:307
where the time goes:
time: 127 us; the launch traced here: 126 us
  waiting for transfers between devices  68.1 us (54%)
  Pallas kernels  22.9 us (18%)
  local copies, waits for them, and re-layouts  19.9 us (16%)
  starting transfers between devices  13.9 us (11%)
    ppermute x6, waiting for transfers between devices, hop(): return lax.ppermute(value, 'leaf', pairs)  59.4 us
    pallas_call x5, Pallas kernels, call(): pl.pallas_call(kernel, out_shape=outs, in_specs=[SMEM_SPEC] + [VMEM_SPEC]...  22.9 us
    unnamed x50, local copies, waits for them, and re-layouts  18 us
    ppermute x6, starting transfers between devices, hop(): return lax.ppermute(value, 'leaf', pairs)  12.2 us
    ppermute x8, waiting for transfers between devices, swap(): return lax.ppermute(value, 'sub', [(0, 1), (1, 0)])  8.69 us
  transfers between devices with their start and end apart: 14, of which 7 were waited for; matrix products, arithmetic and copies ran while one was open for 1% of the time, Pallas kernels for 12%

commit v1 on v0

--- a/solution.py
+++ b/solution.py
@@ -76,7 +76,7 @@
     @pl.when(restart)
     def _():
         x_ref[...] = scale * eye(n)
-        residual()
+        r_ref[...] = eye(n) - scale * e_ref[...]
 
     def fine_go(state):
         step, now, before = state
@@ -198,9 +198,15 @@
     return product(split(jnp.concatenate([w, x], axis=1)), (q[0][...], q[1][...]), NT)
 
 
+def keep(kept, g, be):
+    n = g.shape[0]
+    kept[n : 2 * n, :] = g
+    kept[2 * n :, :] = be
+
+
 def leaf_kernel(
     flags, a_own, a_oth, q_own, q_oth, b_own, b_oth,
-    s_out, load_out, c_out, m_out, g_out, be_out,
+    s_out, load_out, c_out, kept_out,
     ah, al, qh, ql, qth, qtl, ph, pl_, t_ref, e_ref, r_ref,
 ):
     sub = flags[0]
@@ -208,13 +214,12 @@
     load_rotation(sub, q_own, q_oth, (qh, ql), (qth, qtl))
     b = jnp.concatenate(by_half(sub, b_own[...], b_oth[...]), axis=1)
     s, c, g, be = eliminate(
-        (ah, al), (qh, ql), (qth, qtl), split(b), (ph, pl_), t_ref, e_ref, m_out, r_ref
+        (ah, al), (qh, ql), (qth, qtl), split(b), (ph, pl_), t_ref, e_ref, kept_out.at[: q_own.shape[0], :], r_ref
     )
     s_out[...] = s
     pack(sub, s_out, c, load_out)
     c_out[...] = c
-    g_out[...] = g
-    be_out[...] = be
+    keep(kept_out, g, be)
 
 
 def node_kernel(is_root, right_whole, *refs):
@@ -229,11 +234,13 @@
         (left_out, right_out), refs = refs[:2], refs[2:]
         (x_ref, g_ref, s_ref, minv_ref), refs = refs[:4], refs[4:]
     else:
-        (load_out, x_ref, g_ref, be_out), refs = refs[:4], refs[4:]
+        (load_out, kept_out), refs = refs[:2], refs[2:]
         (s_ref,), refs = refs[:1], refs[1:]
     ah, al, qh, ql, qth, qtl, ph, pl_, t_ref, e_ref, r_ref = refs
     sub = flags[0]
     n = e_ref.shape[0]
+    if not is_root:
+        x_ref = kept_out.at[:n, :]
 
     @pl.when(flags[1] != 0)
     def _():
@@ -261,8 +268,8 @@
             (ah, al), (qh, ql), (qth, qtl), split(b), (ph, pl_), t_ref, e_ref, x_ref, r_ref
         )
         s_ref[...] = s
-        g_ref[...] = g
         if is_root:
+            g_ref[...] = g
             invert(s_ref, minv_ref, r_ref)
             x = product(split(c), split(minv_ref[...]))
             v = recover(be, x_ref[...], g_ref[...], x, (qh, ql))
@@ -270,18 +277,18 @@
             right_out[...] = jnp.where(flipped, v[:, :n], v[:, n:])
         else:
             pack(sub, s_ref, c, load_out)
-            be_out[...] = be
-
-
-def down_kernel(flags, be, m, g, xa, xb, q_own, q_oth, left_out, right_out, qh, ql):
+            keep(kept_out, g, be)
+
+
+def down_kernel(flags, kept, xa, xb, q_own, q_oth, left_out, right_out, qh, ql):
     sub = flags[0]
-    n = m.shape[0]
+    n = kept.shape[1]
 
     @pl.when(flags[1] != 0)
     def _():
         load_rotation(sub, q_own, q_oth, (qh, ql), None)
         x = jnp.where(flags[3] != 0, xa[...], xb[...])
-        v = recover(be[...], m[...], g[...], x, (qh, ql))
+        v = recover(kept[2 * n :, :], kept[:n, :], kept[n : 2 * n, :], x, (qh, ql))
         flipped = flags[2] != 0
         left_out[...] = jnp.where(flipped, v[:, n:], v[:, :n])
         right_out[...] = jnp.where(flipped, v[:, :n], v[:, n:])
@@ -336,9 +343,9 @@
     always = jnp.ones((), jnp.int32)
     big = [pltpu.VMEM((full, full), bf16)] * 8
     small = [pltpu.VMEM((full, full), f32)] + [pltpu.VMEM((n, n), f32)] * 2
-    schur, payload, carried, m_leaf, g_leaf, be_leaf = call(
+    schur, payload, carried, kept_leaf = call(
         leaf_kernel,
-        (shape(n, n), shape(*load), shape(count, n), shape(n, n), shape(n, n), shape(count, n)),
+        (shape(n, n), shape(*load), shape(count, n), shape(2 * n + count, n)),
         big + small,
         (flags(always, always), a_own, a_oth, q_own, q_oth, b_own, b_oth),
         "leaf_up",
@@ -366,12 +373,11 @@
                 [pltpu.VMEM((n, n), f32)] * 4 + big + small, args, "root",
             )
         else:
-            payload, m_node, g_node, be_node = call(
+            payload, kept[level] = call(
                 body,
-                (shape(*load), shape(n, n), shape(n, n), shape(count, n)),
+                (shape(*load), shape(2 * n + count, n)),
                 [pltpu.VMEM((n, n), f32)] + big + small, args, "node_up",
             )
-            kept[level] = (be_node, m_node, g_node)
     turn = [pltpu.VMEM((full, full), bf16)] * 2
     for level in range(levels, 0, -1):
         span = 2 ** (level - 1)
@@ -382,7 +388,7 @@
                 down_kernel,
                 (shape(count, n), shape(count, n)),
                 turn,
-                (flags(owner, choice), *kept[level], got_left, got_right, r_own, r_oth),
+                (flags(owner, choice), kept[level], got_left, got_right, r_own, r_oth),
                 "node_down",
             )
         if level == 1:
@@ -400,7 +406,7 @@
         turn,
         (
             jnp.stack([sub.astype(jnp.int32), always, sub.astype(jnp.int32), choice.astype(jnp.int32)]),
-            be_leaf, m_leaf, g_leaf, got_left, got_right, q_own, q_oth,
+            kept_leaf, got_left, got_right, q_own, q_oth,
         ),
         "leaf_down",
     )

time: 127 us -> 122 us (0.961)
  local copies, waits for them, and re-layouts: 19.9 us -> 15.8 us
    unnamed x50 -> x34, local copies, waits for them, and re-layouts: 18 us -> 13.8 us
  transfers between devices with their start and end apart: 14 -> 14, of which waited for: 7 -> 7; matrix products, arithmetic and copies ran while one was open for 1% -> 1% of each run, Pallas kernels for 12% -> 13%
where the time goes in v1:
time: 122 us
  waiting for transfers between devices  67.9 us (56%)
  Pallas kernels  22.9 us (19%)
  local copies, waits for them, and re-layouts  15.8 us (13%)
  starting transfers between devices  13.8 us (11%)
    ppermute x6, waiting for transfers between devices, hop(): return lax.ppermute(value, 'leaf', pairs)  59.2 us
    pallas_call x5, Pallas kernels, call(): pl.pallas_call(kernel, out_shape=outs, in_specs=[SMEM_SPEC] + [VMEM_SPEC]...  22.9 us
    unnamed x34, local copies, waits for them, and re-layouts  13.8 us
    ppermute x6, starting transfers between devices, hop(): return lax.ppermute(value, 'leaf', pairs)  12.2 us
    ppermute x8, waiting for transfers between devices, swap(): return lax.ppermute(value, 'sub', [(0, 1), (1, 0)])  8.69 us
  transfers between devices with their start and end apart: 14, of which 7 were waited for; matrix products, arithmetic and copies ran while one was open for 1% of the time, Pallas kernels for 13%

profile of v1, /device:TPU:0, one launch (start us, length us, event | category | flops | bytes accessed | tf_op | source)
XLA Modules:
  0.0 121.6 jit_solution(1022007750379596758)
XLA Ops:
  0.0 0.5 collective-permute-start
  0.5 0.0 collective-permute-start.1
  0.5 0.5 collective-permute-start.5
  1.0 1.0 constant_dynamic-slice_fusion
  2.1 0.1 collective-permute-start.2
  2.8 0.1 pad_add_fusion.2.flags
  2.9 3.8 %collective-permute-done.2.b_oth = f32[64,384]{1,0:T(8,128)S(1)} collective-permute-done((f32[64,384]{1,0:T(8,128)S(1)}, f32[64,384]{1,0:T(8,128)S(1)}, u32[]{:S(2)}, u32[]{:S(2)}) %collective-permute-start.2) | collective-permute-done | bytes 98336 | tf_op jit(solution)/shard_map/ppermute | solution.py:314
  6.7 0.0 collective-permute-done.a_oth
  6.7 0.0 copy-start.10
  6.7 1.0 copy-done.10
  7.7 0.0 collective-permute-done.1.q_oth
  7.7 0.0 copy-start.1
  7.7 1.3 %copy-done.1 = f32[1,384,768]{2,1,0:T(8,128)S(1)} copy-done((f32[1,384,768]{2,1,0:T(8,128)S(1)}, f32[1,384,768]{2,1,0:T(8,128)}, u32[]{:S(2)}) %copy-start.1) | copy-done | bytes 1179672
  9.0 0.0 copy-start.9
  9.0 1.3 %copy-done.9 = f32[1,384,768]{2,1,0:T(8,128)S(1)} copy-done((f32[1,384,768]{2,1,0:T(8,128)S(1)}, f32[1,384,768]{2,1,0:T(8,128)}, u32[]{:S(2)}) %copy-start.9) | copy-done | bytes 1179672
  10.3 0.0 copy-start.11
  10.3 1.3 %copy-done.11 = f32[384,768]{1,0:T(8,128)S(1)} copy-done((f32[384,768]{1,0:T(8,128)S(1)}, f32[384,768]{1,0:T(8,128)}, u32[]{:S(2)}) %copy-start.11) | copy-done | bytes 1179672
  11.5 0.0 copy-start
  11.5 15.7 %leaf_up.1 = (f32[384,384]{1,0:T(8,128)S(1)}, f32[576,128]{1,0:T(8,128)S(1)}, f32[64,384]{1,0:T(8,128)S(1)}, f32[832,384]{1,0:T(8,128)S(1)}) custom-call(s32[4]{0:T(128)S(1)} %pad_add_fusion.2.flags, f32[384,768]{1,0:T(8,128)S(1)} %bitcast.27, f32[384,768]{1,0:T(8,128)S(1)} %copy-done.11, f32[384,768]{1,0:T(8,128)S(1)} %bitcast.22, ...), custom_call_target="tpu_custom_call" | custom-call | tf_op jit(solution)/shard_map/leaf_up/pallas_call | solution.py:302
  27.2 0.0 copy-start.5
  27.2 1.1 copy-done.5
  28.3 0.0 copy-start.12
  28.3 0.8 copy-done.12
  29.1 0.6 copy-done.14
  29.8 5.5 %collective-permute-start.3 = (f32[576,128]{1,0:T(8,128)S(1)}, f32[576,128]{1,0:T(8,128)}, u32[]{:S(2)}, u32[]{:S(2)}) collective-permute-start(f32[576,128]{1,0:T(8,128)S(1)} %get-tuple-element.18), channel_id=1, source_target_pairs={{0,4},{8,12},{1,5},{9,13},{2,6},{10,14},{3,7},{11,15},{16,20},{24,... | collective-permute-start | bytes 884744 | tf_op jit(solution)/shard_map/ppermute | solution.py:318
  35.3 5.8 %collective-permute-done.3.refs_1_ = f32[576,128]{1,0:T(8,128)} collective-permute-done((f32[576,128]{1,0:T(8,128)S(1)}, f32[576,128]{1,0:T(8,128)}, u32[]{:S(2)}, u32[]{:S(2)}) %collective-permute-start.3) | collective-permute-done | bytes 294944 | tf_op jit(solution)/shard_map/ppermute | solution.py:318
  41.2 0.0 collective-permute-start.4
  41.2 0.1 pad_add_fusion.1
  41.3 0.0 collective-permute-done.5.refs_7_.q_oth
  41.3 1.8 %collective-permute-done.4.refs_2_ = f32[576,128]{1,0:T(8,128)} collective-permute-done((f32[576,128]{1,0:T(8,128)}, f32[576,128]{1,0:T(8,128)}, u32[]{:S(2)}, u32[]{:S(2)}) %collective-permute-start.4) | collective-permute-done | bytes 294944 | tf_op jit(solution)/shard_map/ppermute | solution.py:314
  43.1 0.0 copy-done
  43.1 1.1 copy-done.3
  44.2 1.1 copy-done.13
  45.2 0.9 copy-done.15
  46.1 1.3 %node_up.1 = (f32[576,128]{1,0:T(8,128)S(1)}, f32[832,384]{1,0:T(8,128)S(1)}) custom-call(s32[4]{0:T(128)S(1)} %get-tuple-element.29.refs_0_, f32[576,128]{1,0:T(8,128)} %collective-permute-done.3.refs_1_, f32[576,128]{1,0:T(8,128)} %collective-permute-done.4.refs_2_, f32[384,384]{1,0:T(8,128)S(1)} %copy-done.13, f32[64,384]{1,0:T(8,128)S(1)} %copy-done.15, ...), custom_call_target="tpu_custom_call" | custom-call | tf_op jit(solution)/shard_map/node_up/pallas_call | solution.py:302
  47.4 0.0 copy-start.7
  47.4 1.1 copy-done.7
  48.5 1.4 %collective-permute-start.8 = (f32[576,128]{1,0:T(8,128)S(1)}, f32[576,128]{1,0:T(8,128)}, u32[]{:S(2)}, u32[]{:S(2)}) collective-permute-start(f32[576,128]{1,0:T(8,128)S(1)} %get-tuple-element.22), channel_id=1, source_target_pairs={{12,8},{13,9},{14,10},{15,11},{28,24},{29,25},{30,26},{31,27}} | collective-permute-start | bytes 884744 | tf_op jit(solution)/shard_map/ppermute | solution.py:318
  49.9 1.4 %collective-permute-start.6 = (f32[576,128]{1,0:T(8,128)S(1)}, f32[576,128]{1,0:T(8,128)}, u32[]{:S(2)}, u32[]{:S(2)}) collective-permute-start(f32[576,128]{1,0:T(8,128)S(1)} %get-tuple-element.22), channel_id=1, source_target_pairs={{4,8},{5,9},{6,10},{7,11},{20,24},{21,25},{22,26},{23,27}} | collective-permute-start | bytes 884744 | tf_op jit(solution)/shard_map/ppermute | solution.py:318
  51.2 0.0 collective-permute-done.8.refs_3_
  51.2 0.1 collective-permute-start.9
  51.4 0.0 collective-permute-done.6.refs_1_
  51.4 0.4 collective-permute-start.7
  51.7 0.1 pad_add_fusion.refs_0_
  51.8 1.3 %collective-permute-done.9.refs_4_ = f32[576,128]{1,0:T(8,128)} collective-permute-done((f32[576,128]{1,0:T(8,128)}, f32[576,128]{1,0:T(8,128)}, u32[]{:S(2)}, u32[]{:S(2)}) %collective-permute-start.9) | collective-permute-done | bytes 294944 | tf_op jit(solution)/shard_map/ppermute | solution.py:314
  53.2 0.4 collective-permute-done.7.refs_2_
  53.6 1.1 copy-done.4
  54.6 2.2 %root.1 = (f32[64,384]{1,0:T(8,128)}, f32[64,384]{1,0:T(8,128)}) custom-call(s32[4]{0:T(128)S(1)} %pad_add_fusion.refs_0_, f32[576,128]{1,0:T(8,128)} %collective-permute-done.6.refs_1_, f32[576,128]{1,0:T(8,128)} %collective-permute-done.7.refs_2_, f32[576,128]{1,0:T(8,128)} %collective-permute-done.8.refs_3_, f32[576,128]{1,0:T(8,128)} %collective-permute-done.9.refs_4_, ...), custom_call_target="tpu_custom_call" | custom-call | tf_op jit(solution)/shard_map/root/pallas_call | solution.py:302
  56.8 1.3 %collective-permute-start.10 = (f32[64,384]{1,0:T(8,128)}, f32[64,384]{1,0:T(8,128)}, u32[]{:S(2)}, u32[]{:S(2)}) collective-permute-start(f32[64,384]{1,0:T(8,128)} %get-tuple-element.23), channel_id=1, source_target_pairs={{8,4},{9,5},{10,6},{11,7},{24,20},{25,21},{26,22},{27,23}} | collective-permute-start | bytes 294920 | tf_op jit(solution)/shard_map/ppermute | solution.py:318
  58.1 1.3 %collective-permute-start.11 = (f32[64,384]{1,0:T(8,128)}, f32[64,384]{1,0:T(8,128)}, u32[]{:S(2)}, u32[]{:S(2)}) collective-permute-start(f32[64,384]{1,0:T(8,128)} %get-tuple-element.24), channel_id=1, source_target_pairs={{8,12},{9,13},{10,14},{11,15},{24,28},{25,29},{26,30},{27,31}} | collective-permute-start | bytes 294920 | tf_op jit(solution)/shard_map/ppermute | solution.py:318
  59.4 0.1 pad_add_fusion.5.flags
  59.5 0.0 collective-permute-done.10.xa
  59.5 0.0 collective-permute-done.11.xb
  59.5 1.3 %copy-done.8 = f32[832,384]{1,0:T(8,128)S(1)} copy-done((f32[832,384]{1,0:T(8,128)S(1)}, f32[832,384]{1,0:T(8,128)}, u32[]{:S(2)}) %copy-start.8) | copy-done | bytes 1277976
  60.8 1.1 node_down.1
  61.9 1.3 %collective-permute-start.12 = (f32[64,384]{1,0:T(8,128)S(1)}, f32[64,384]{1,0:T(8,128)S(1)}, u32[]{:S(2)}, u32[]{:S(2)}) collective-permute-start(f32[64,384]{1,0:T(8,128)S(1)} %get-tuple-element.25), channel_id=1, source_target_pairs={{4,0},{12,8},{5,1},{13,9},{6,2},{14,10},{7,3},{15,11},{20,16},{28,... | collective-permute-start | bytes 294920 | tf_op jit(solution)/shard_map/ppermute | solution.py:318
  63.2 0.1 pad_add_fusion.3.flags
  63.3 53.3 %collective-permute-done.12.xa = f32[64,384]{1,0:T(8,128)S(1)} collective-permute-done((f32[64,384]{1,0:T(8,128)S(1)}, f32[64,384]{1,0:T(8,128)S(1)}, u32[]{:S(2)}, u32[]{:S(2)}) %collective-permute-start.12) | collective-permute-done | bytes 98336 | tf_op jit(solution)/shard_map/ppermute | solution.py:318
  116.6 0.0 copy-done.2
  116.6 0.0 copy-done.6
  116.6 2.6 %leaf_down.1 = (f32[64,384]{1,0:T(8,128)S(1)}, f32[64,384]{1,0:T(8,128)S(1)}) custom-call(s32[4]{0:T(128)S(1)} %pad_add_fusion.3.flags, f32[832,384]{1,0:T(8,128)S(1)} %copy-done.6, f32[64,384]{1,0:T(8,128)S(1)} %collective-permute-done.12.xa, f32[64,384]{1,0:T(8,128)S(1)} %get-tuple-element.26.xb, f32[384,768]{1,0:T(8,128)S(1)} %bitcast.23, ...), custom_call_target="tpu_custom_call" | custom-call | tf_op jit(solution)/shard_map/leaf_down/pallas_call | solution.py:302
  119.3 0.1 collective-permute-start.13
  119.4 1.3 %collective-permute-done.13 = f32[64,384]{1,0:T(8,128)S(1)} collective-permute-done((f32[64,384]{1,0:T(8,128)S(1)}, f32[64,384]{1,0:T(8,128)S(1)}, u32[]{:S(2)}, u32[]{:S(2)}) %collective-permute-start.13) | collective-permute-done | bytes 98336 | tf_op jit(solution)/shard_map/ppermute | solution.py:314
  120.7 0.9 copy.7
  (11 shorter events, 0.0 us)
Async XLA Ops:
  0.0 6.7 %collective-permute-start = (f32[384,768]{1,0:T(8,128)}, f32[384,768]{1,0:T(8,128)S(1)}, u32[]{:S(2)}, u32[]{:S(2)}) collective-permute-start(f32[384,768]{1,0:T(8,128)} %bitcast.26), channel_id=1, source_target_pairs={{0,1},{1,0},{2,3},{3,2},{4,5},{5,4},{6,7},{7,6},{8,9},{9,8},{10,11... | collective-permute-start | bytes 3538952 | tf_op jit(solution)/shard_map/ppermute | solution.py:314
  0.5 7.2 %collective-permute-start.1 = (f32[384,768]{1,0:T(8,128)}, f32[384,768]{1,0:T(8,128)S(1)}, u32[]{:S(2)}, u32[]{:S(2)}) collective-permute-start(f32[384,768]{1,0:T(8,128)} %bitcast.21), channel_id=1, source_target_pairs={{0,1},{1,0},{2,3},{3,2},{4,5},{5,4},{6,7},{7,6},{8,9},{9,8},{10,11... | collective-permute-start | bytes 3538952 | tf_op jit(solution)/shard_map/ppermute | solution.py:314
  0.5 40.7 %collective-permute-start.5 = (f32[384,768]{1,0:T(8,128)}, f32[384,768]{1,0:T(8,128)S(1)}, u32[]{:S(2)}, u32[]{:S(2)}) collective-permute-start(f32[384,768]{1,0:T(8,128)} %bitcast.17), channel_id=1, source_target_pairs={{0,1},{1,0},{2,3},{3,2},{4,5},{5,4},{6,7},{7,6},{8,9},{9,8},{10,11... | collective-permute-start | bytes 3538952 | tf_op jit(solution)/shard_map/ppermute | solution.py:314
  2.1 4.6 %collective-permute-start.2 = (f32[64,384]{1,0:T(8,128)S(1)}, f32[64,384]{1,0:T(8,128)S(1)}, u32[]{:S(2)}, u32[]{:S(2)}) collective-permute-start(f32[64,384]{1,0:T(8,128)S(1)} %bitcast.30), channel_id=1, source_target_pairs={{0,1},{1,0},{2,3},{3,2},{4,5},{5,4},{6,7},{7,6},{8,9},{9,8},{10,11... | collective-permute-start | bytes 294920 | tf_op jit(solution)/shard_map/ppermute | solution.py:314
  6.7 1.0 copy-start.10
  7.7 1.3 %copy-start.1 = (f32[1,384,768]{2,1,0:T(8,128)S(1)}, f32[1,384,768]{2,1,0:T(8,128)}, u32[]{:S(2)}) copy-start(f32[1,384,768]{2,1,0:T(8,128)} %param.8) | copy-start | bytes 3538948
  9.0 1.3 %copy-start.9 = (f32[1,384,768]{2,1,0:T(8,128)S(1)}, f32[1,384,768]{2,1,0:T(8,128)}, u32[]{:S(2)}) copy-start(f32[1,384,768]{2,1,0:T(8,128)} %param.7) | copy-start | bytes 3538948
  10.3 1.3 %copy-start.11 = (f32[384,768]{1,0:T(8,128)S(1)}, f32[384,768]{1,0:T(8,128)}, u32[]{:S(2)}) copy-start(f32[384,768]{1,0:T(8,128)} %copy-done.10) | copy-start | bytes 3538948
  11.5 31.6 %copy-start = (f32[1,384,768]{2,1,0:T(8,128)S(1)}, f32[1,384,768]{2,1,0:T(8,128)}, u32[]{:S(2)}) copy-start(f32[1,384,768]{2,1,0:T(8,128)} %param.9) | copy-start | bytes 3538948
  27.2 1.1 copy-start.5
  28.3 0.8 copy-start.12
  29.1 0.6 copy-start.14
  29.8 11.4 %collective-permute-start.3 = (f32[576,128]{1,0:T(8,128)S(1)}, f32[576,128]{1,0:T(8,128)}, u32[]{:S(2)}, u32[]{:S(2)}) collective-permute-start(f32[576,128]{1,0:T(8,128)S(1)} %get-tuple-element.18), channel_id=1, source_target_pairs={{0,4},{8,12},{1,5},{9,13},{2,6},{10,14},{3,7},{11,15},{16,20},{24,... | collective-permute-start | bytes 884744 | tf_op jit(solution)/shard_map/ppermute | solution.py:318
  41.2 1.9 %collective-permute-start.4 = (f32[576,128]{1,0:T(8,128)}, f32[576,128]{1,0:T(8,128)}, u32[]{:S(2)}, u32[]{:S(2)}) collective-permute-start(f32[576,128]{1,0:T(8,128)} %collective-permute-done.3.refs_1_), channel_id=1, source_target_pairs={{0,1},{1,0},{2,3},{3,2},{4,5},{5,4},{6,7},{7,6},{8,9},{9,8},{10,11... | collective-permute-start | bytes 884744 | tf_op jit(solution)/shard_map/ppermute | solution.py:314
  43.1 1.1 copy-start.3
  44.2 1.1 copy-start.13
  45.2 0.9 copy-start.15
  47.4 1.1 copy-start.7
  48.5 2.7 %collective-permute-start.8 = (f32[576,128]{1,0:T(8,128)S(1)}, f32[576,128]{1,0:T(8,128)}, u32[]{:S(2)}, u32[]{:S(2)}) collective-permute-start(f32[576,128]{1,0:T(8,128)S(1)} %get-tuple-element.22), channel_id=1, source_target_pairs={{12,8},{13,9},{14,10},{15,11},{28,24},{29,25},{30,26},{31,27}} | collective-permute-start | bytes 884744 | tf_op jit(solution)/shard_map/ppermute | solution.py:318
  49.9 1.5 %collective-permute-start.6 = (f32[576,128]{1,0:T(8,128)S(1)}, f32[576,128]{1,0:T(8,128)}, u32[]{:S(2)}, u32[]{:S(2)}) collective-permute-start(f32[576,128]{1,0:T(8,128)S(1)} %get-tuple-element.22), channel_id=1, source_target_pairs={{4,8},{5,9},{6,10},{7,11},{20,24},{21,25},{22,26},{23,27}} | collective-permute-start | bytes 884744 | tf_op jit(solution)/shard_map/ppermute | solution.py:318
  51.2 1.9 %collective-permute-start.9 = (f32[576,128]{1,0:T(8,128)}, f32[576,128]{1,0:T(8,128)}, u32[]{:S(2)}, u32[]{:S(2)}) collective-permute-start(f32[576,128]{1,0:T(8,128)} %collective-permute-done.8.refs_3_), channel_id=1, source_target_pairs={{0,1},{1,0},{2,3},{3,2},{4,5},{5,4},{6,7},{7,6},{8,9},{9,8},{10,11... | collective-permute-start | bytes 884744 | tf_op jit(solution)/shard_map/ppermute | solution.py:314
  51.4 2.2 %collective-permute-start.7 = (f32[576,128]{1,0:T(8,128)}, f32[576,128]{1,0:T(8,128)}, u32[]{:S(2)}, u32[]{:S(2)}) collective-permute-start(f32[576,128]{1,0:T(8,128)} %collective-permute-done.6.refs_1_), channel_id=1, source_target_pairs={{0,1},{1,0},{2,3},{3,2},{4,5},{5,4},{6,7},{7,6},{8,9},{9,8},{10,11... | collective-permute-start | bytes 884744 | tf_op jit(solution)/shard_map/ppermute | solution.py:314
  53.6 1.1 copy-start.4
  56.8 2.7 %collective-permute-start.10 = (f32[64,384]{1,0:T(8,128)}, f32[64,384]{1,0:T(8,128)}, u32[]{:S(2)}, u32[]{:S(2)}) collective-permute-start(f32[64,384]{1,0:T(8,128)} %get-tuple-element.23), channel_id=1, source_target_pairs={{8,4},{9,5},{10,6},{11,7},{24,20},{25,21},{26,22},{27,23}} | collective-permute-start | bytes 294920 | tf_op jit(solution)/shard_map/ppermute | solution.py:318
  58.1 1.4 %collective-permute-start.11 = (f32[64,384]{1,0:T(8,128)}, f32[64,384]{1,0:T(8,128)}, u32[]{:S(2)}, u32[]{:S(2)}) collective-permute-start(f32[64,384]{1,0:T(8,128)} %get-tuple-element.24), channel_id=1, source_target_pairs={{8,12},{9,13},{10,14},{11,15},{24,28},{25,29},{26,30},{27,31}} | collective-permute-start | bytes 294920 | tf_op jit(solution)/shard_map/ppermute | solution.py:318
  59.5 1.3 %copy-start.8 = (f32[832,384]{1,0:T(8,128)S(1)}, f32[832,384]{1,0:T(8,128)}, u32[]{:S(2)}) copy-start(f32[832,384]{1,0:T(8,128)} %copy-done.7) | copy-start | bytes 3833860
  60.8 55.8 %copy-start.2 = (f32[1,384,768]{2,1,0:T(8,128)S(1)}, f32[1,384,768]{2,1,0:T(8,128)}, u32[]{:S(2)}) copy-start(f32[1,384,768]{2,1,0:T(8,128)} %param.8) | copy-start | bytes 3538948
  60.8 55.8 %copy-start.6 = (f32[832,384]{1,0:T(8,128)S(1)}, f32[832,384]{1,0:T(8,128)}, u32[]{:S(2)}) copy-start(f32[832,384]{1,0:T(8,128)} %copy-done.5) | copy-start | bytes 3833860
  61.9 54.7 %collective-permute-start.12 = (f32[64,384]{1,0:T(8,128)S(1)}, f32[64,384]{1,0:T(8,128)S(1)}, u32[]{:S(2)}, u32[]{:S(2)}) collective-permute-start(f32[64,384]{1,0:T(8,128)S(1)} %get-tuple-element.25), channel_id=1, source_target_pairs={{4,0},{12,8},{5,1},{13,9},{6,2},{14,10},{7,3},{15,11},{20,16},{28,... | collective-permute-start | bytes 294920 | tf_op jit(solution)/shard_map/ppermute | solution.py:318
  119.3 1.4 %collective-permute-start.13 = (f32[64,384]{1,0:T(8,128)S(1)}, f32[64,384]{1,0:T(8,128)S(1)}, u32[]{:S(2)}, u32[]{:S(2)}) collective-permute-start(f32[64,384]{1,0:T(8,128)S(1)} %get-tuple-element.28), channel_id=1, source_target_pairs={{0,1},{1,0},{2,3},{3,2},{4,5},{5,4},{6,7},{7,6},{8,9},{9,8},{10,11... | collective-permute-start | bytes 294920 | tf_op jit(solution)/shard_map/ppermute | solution.py:314
